TPU v7x, 512 devices: a whole 4x8x8 slice. The times are simulated.
512 devices in a mesh: grp: 4 (over z_hi, core), wide: 128 (over z_lo, x, y).
Axes of the slice: x: 4, y: 8, z: 8 (z_hi: 2, z_lo: 4; z = z_hi * 4 + z_lo), core: 2. Of those that a mesh axis runs over, the one named last changes fastest.
Arguments:
- images: bfloat16 [2048, 256, 2048], P(('grp', 'wide')), may hold values from -6 to 6
- legendre_real: float32 [128, 128], replicated, may hold values from -0.375 to 0.375
- legendre_imag: float32 [128, 128], replicated, may hold values from -0.375 to 0.375
- amplitudes: float32 [128, 256, 128], P('wide'), may hold values from -6 to 6
Outputs:
- projected: float32 [128, 256, 128], P('wide', 'grp')
All inputs are finite; a program needn't handle non-finite values.
Results may differ from a plain program's by a relative error of at most 0.0023.
Values may be sent and summed in bfloat16 or wider, within the bound.
No kernel may reach another device: no remote copies, remote signals or barrier semaphores. Data moves between devices by JAX's collectives and lax.ppermute only.
A program may use at most 64 MiB of HBM per device.

v0:
```python
import math
import jax
import jax.numpy as jnp
from jax import lax
from jax.sharding import PartitionSpec as P

HARMS = 128


def harmonic_rows(points, count):
    angle_idx = jnp.arange(points, dtype=jnp.int32)
    harm_idx = jnp.arange(count, dtype=jnp.int32)
    product = harm_idx[:, None] * angle_idx[None, :] % points
    phase = product.astype(jnp.float32) * (2.0 * math.pi / points)
    norm_scale = 1.0 / math.sqrt(points)
    both = jnp.stack([jnp.cos(phase) * norm_scale, -jnp.sin(phase) * norm_scale], axis=1)
    return both.reshape(count * 2, points).astype(jnp.bfloat16)


def invert_harms(stacked, legendre_real, legendre_imag):
    result = jnp.dot(legendre_real, stacked[:, 0], precision=lax.Precision.HIGHEST)
    return result + jnp.dot(legendre_imag, stacked[:, 1], precision=lax.Precision.HIGHEST)


def body(images, legendre_real, legendre_imag, amplitudes):
    local_img, radii, points = images.shape
    table_rows = harmonic_rows(points, HARMS)
    flat_images = images.reshape(local_img * radii, points)
    spectra = lax.dot_general(
        table_rows, flat_images, (((1,), (1,)), ((), ())), preferred_element_type=jnp.float32
    )
    spectra = spectra.astype(jnp.bfloat16).reshape(HARMS, 2, local_img, radii)
    pooled = lax.all_to_all(spectra, "wide", split_axis=0, concat_axis=2, tiled=True)
    total_img = pooled.shape[2] * lax.axis_size("grp")
    gram = jnp.einsum("kanr,kbns->kabrs", pooled, pooled, preferred_element_type=jnp.float32)
    real_part = (gram[:, 0, 0] + gram[:, 1, 1]) / total_img
    imag_part = (gram[:, 1, 0] - gram[:, 0, 1]) / total_img
    corr = jnp.stack([real_part, imag_part], axis=1)
    own_harms = corr.shape[0]
    own_degrees = amplitudes.shape[0]
    groups = lax.axis_size("grp")
    summed = lax.psum_scatter(corr, "grp", scatter_dimension=2, tiled=True)
    flat = summed.reshape(own_harms, 2, radii // groups * radii)
    every_harm = lax.all_to_all(flat, "wide", split_axis=2, concat_axis=0, tiled=True)
    degree_part = invert_harms(every_harm, legendre_real, legendre_imag)
    mine = lax.all_to_all(degree_part, "wide", split_axis=0, concat_axis=1, tiled=True)
    inverted = mine.reshape(own_degrees, radii // groups, radii)
    return jnp.einsum("lrs,lsk->lrk", inverted, amplitudes, precision=lax.Precision.HIGHEST)


def solution(mesh):
    return jax.shard_map(
        body,
        mesh=mesh,
        in_specs=(P(("grp", "wide"), None, None), P(), P(), P("wide", None, None)),
        out_specs=P("wide", "grp", None),
        check_vma=False,
    )
```

profile of v0, /device:TPU:2, one launch (start us, length us, event | category | flops | bytes accessed | tf_op | source)
XLA Modules:
  0.0 285.0 jit_solution(9286189481164600383)
XLA Ops:
  6.5 4.3 %multiply_convert_fusion = (bf16[128,1,2048]{2,0,1:T(8,128)(2,1)S(1)}, bf16[128,1,2048]{2,0,1:T(8,128)(2,1)S(1)}) fusion(), kind=kLoop, calls=%fused_computation.12 | loop fusion | flops 4980736 | bytes 1048576 | tf_op jit(solution)/shard_map/convert.1
  11.0 1.1 copy.43
  12.1 0.4 convert_element_type.30
  12.5 3.5 %convolution_convert_fusion = bf16[256,1024]{1,0:T(8,128)(2,1)S(1)} fusion(bf16[256,2048]{1,0:T(8,128)(2,1)S(1)} %convert_element_type.30, bf16[1024,2048]{1,0:T(8,128)(2,1)} %bitcast.73), kind=kOutput, calls=%fused_computation.4 | convolution fusion | flops 1074003968 | bytes 5767168 | tf_op jit(solution)/shard_map/dot_general | solution.py:29
  16.0 0.4 reshape.176
  16.4 35.2 %all_to_all.46 = bf16[128,2,4,256]{3,2,1,0:T(4,128)(2,1)S(1)} all-to-all(bf16[128,2,4,256]{3,2,1,0:T(4,128)(2,1)S(1)} %reshape.176), channel_id=1, replica_groups=mesh['grp'=4,'wide'=128] {'wide'}, dimensions={0} | all-to-all | bytes 1048576 | tf_op jit(solution)/shard_map/all_to_all | solution.py:33
  51.6 0.5 copy.55
  52.0 0.5 convolution_bitcast_fusion
  52.7 1.0 copy.49
  53.7 1.3 dynamic-slice
  55.6 59.9 %all-reduce.3.cloned.1.call-done = f32[1,2,256,256]{3,1,0,2:T(2,128)} async-done(((f32[1,2,256,256]{3,1,0,2:T(2,128)}), f32[1,2,256,256]{3,1,0,2:T(2,128)}) %all-reduce.3.cloned.1.call-update) | async-done | bytes 524304
  115.6 0.9 constant_dynamic-slice_fusion
  116.5 12.0 %copy.50 = f32[1,2,16384]{1,0,2:T(1,128)} copy(f32[1,2,16384]{2,1,0:T(2,128)S(1)} %bitcast.70) | data formatting | bytes 262144 | tf_op jit(solution)/shard_map/reshape | solution.py:43
  128.5 0.5 broadcast.138
  129.0 74.5 %reduce.4 = f32[16384,2]{1,0:T(8,128)} reduce(f32[16384,1,2]{2,1,0:T(1,128)} %bitcast.68, f32[]{:T(128)} %broadcast.138), dimensions={1}, to_apply=%bitcast.61.reduce_sub_computation | reduce | bytes 262148
  203.5 7.6 %reshape.194 = f32[128,1,256]{2,1,0:T(1,128)S(1)} reshape(f32[16384,2]{1,0:T(8,128)} %reduce.4) | data formatting | bytes 262144
  211.1 24.9 %all_to_all.47 = f32[128,1,256]{2,1,0:T(1,128)S(1)} all-to-all(f32[128,1,256]{2,1,0:T(1,128)S(1)} %reshape.194), channel_id=1, replica_groups=mesh['grp'=4,'wide'=128] {'wide'}, dimensions={0} | all-to-all | bytes 262144 | tf_op jit(solution)/shard_map/all_to_all | solution.py:44
  236.0 1.0 reduce.5
  236.9 14.9 %reshape.195 = f32[16384,1,2]{2,1,0:T(1,128)} reshape(f32[128,256]{1,0:T(8,128)S(1)} %reduce.5) | data formatting | bytes 262144
  251.8 5.2 %copy.56 = f32[1,2,128,128]{3,2,1,0:T(8,128)S(1)} copy(f32[1,2,128,128]{1,3,2,0:T(8,128)} %bitcast.69) | data formatting | bytes 262144 | tf_op jit(solution)/shard_map/all_to_all | solution.py:44
  257.8 18.1 %all_to_all.48 = f32[128,1,128]{2,1,0:T(1,128)S(1)} all-to-all(f32[128,1,128]{2,1,0:T(1,128)S(1)} %copy.52), channel_id=1, replica_groups=mesh['grp'=4,'wide'=128] {'wide'}, dimensions={0} | all-to-all | bytes 131072 | tf_op jit(solution)/shard_map/all_to_all | solution.py:46
  275.9 0.5 broadcast.137
  276.4 0.8 reduce.3
  277.3 0.8 convolution_bitcast_fusion.1
  (16 shorter events, 0.9 us)
Async XLA Ops:
  6.5 270.7 %copy-start = (f32[1,256,128]{2,1,0:T(8,128)S(1)}, f32[1,256,128]{2,1,0:T(8,128)}, u32[]{:S(2)}) copy-start(f32[1,256,128]{2,1,0:T(8,128)} %param.7) | copy-start | bytes 393220
  6.5 109.0 %all-reduce.3.cloned.1.call-start = ((), (), s32[]{:S(2)}) async-start(), calls=%async_computation.3 | async-start | bytes 1048576
  251.8 5.3 %copy-start.1 = (f32[128,128]{1,0:T(8,128)S(1)}, f32[128,128]{1,0:T(8,128)}, u32[]{:S(2)}) copy-start(f32[128,128]{1,0:T(8,128)} %param.5) | copy-start | bytes 196612
  251.8 5.6 %copy-start.2 = (f32[128,128]{1,0:T(8,128)S(1)}, f32[128,128]{1,0:T(8,128)}, u32[]{:S(2)}) copy-start(f32[128,128]{1,0:T(8,128)} %param.6) | copy-start | bytes 196612
Sparse Core Ops, SparseCore 0:
  53.8 61.6 all-reduce.2
where the time goes:
time: 285 us
  other arithmetic  80.7 us (28%)
  blocking collectives  78.2 us (27%)
  waiting for transfers between devices  60 us (21%)
  local copies, waits for them, and re-layouts  46.5 us (16%)
  between operations  14.2 us (5%)
  matrix products  5.35 us (2%)
    unnamed x1, other arithmetic  74.5 us
    unnamed x2, waiting for transfers between devices  60 us
    all_to_all x1, blocking collectives, body(): lax.all_to_all(spectra, 'wide', split_axis=0, concat_axis=2, tiled=True)  35.2 us
    unnamed x11, local copies, waits for them, and re-layouts  25.2 us
    all_to_all x1, blocking collectives, body(): lax.all_to_all(flat, 'wide', split_axis=2, concat_axis=0, tiled=True)  24.9 us
    all_to_all x1, blocking collectives, body(): lax.all_to_all(degree_part, 'wide', split_axis=0, concat_axis=1, tiled=True)  18.1 us
    reshape x1, local copies, waits for them, and re-layouts, body(): flat = summed.reshape(own_harms, 2, radii // groups * radii)  12 us
  transfers between devices with their start and end apart: 1, of which 1 were waited for; matrix products, arithmetic and copies ran while one was open for 0% of the time, Pallas kernels for 0%

commit v1 on v0

--- a/solution.py
+++ b/solution.py
@@ -41,7 +41,10 @@
     groups = lax.axis_size("grp")
     summed = lax.psum_scatter(corr, "grp", scatter_dimension=2, tiled=True)
     flat = summed.reshape(own_harms, 2, radii // groups * radii)
-    every_harm = lax.all_to_all(flat, "wide", split_axis=2, concat_axis=0, tiled=True)
+    every_harm = jnp.concatenate(
+        lax.all_to_all(jnp.stack(jnp.split(flat, lax.axis_size("wide"), axis=2)), "wide", 0, 0),
+        axis=0,
+    )
     degree_part = invert_harms(every_harm, legendre_real, legendre_imag)
     mine = lax.all_to_all(degree_part, "wide", split_axis=0, concat_axis=1, tiled=True)
     inverted = mine.reshape(own_degrees, radii // groups, radii)

time: 285 us -> 171 us (0.60)
  other arithmetic: 80.7 us -> 5.34 us
  local copies, waits for them, and re-layouts: 46.5 us -> 7.41 us
    unnamed x1 -> x0, other arithmetic: 74.5 us -> none
    unnamed x11 -> x135, local copies, waits for them, and re-layouts: 25.2 us -> 3.32 us
    reshape x1 -> x0, local copies, waits for them, and re-layouts: 12 us -> none  [body(): flat = summed.reshape(own_harms, 2, radii // groups * radii)]
    all_to_all x1 -> x0, local copies, waits for them, and re-layouts: 5.25 us -> none  [body(): lax.all_to_all(flat, 'wide', split_axis=2, concat_axis=0, tiled=True)]
  transfers between devices with their start and end apart: 1 -> 1, of which waited for: 1 -> 1; matrix products, arithmetic and copies ran while one was open for 0% -> 1% of each run, Pallas kernels for 0% -> 0%
where the time goes in v1:
time: 171 us
  blocking collectives  78.2 us (46%)
  waiting for transfers between devices  60 us (35%)
  between operations  14.6 us (9%)
  local copies, waits for them, and re-layouts  7.41 us (4%)
  other arithmetic  5.34 us (3%)
  matrix products  5.34 us (3%)
    unnamed x2, waiting for transfers between devices  60 us
    all_to_all x1, blocking collectives, body(): lax.all_to_all(spectra, 'wide', split_axis=0, concat_axis=2, tiled=True)  35.2 us
    all_to_all x1, blocking collectives, body(): lax.all_to_all(jnp.stack(jnp.split(flat, lax.axis_size('wide'), axis=2)),...  24.9 us
    all_to_all x1, blocking collectives, body(): lax.all_to_all(degree_part, 'wide', split_axis=0, concat_axis=1, tiled=True)  18.1 us
    another operation x1, other arithmetic  4.33 us
    dot_general x1, matrix products, body(): lax.dot_general(table_rows, flat_images, (((1,), (1,)), ((), ())), prefer...  3.47 us
  transfers between devices with their start and end apart: 1, of which 1 were waited for; matrix products, arithmetic and copies ran while one was open for 1% of the time, Pallas kernels for 0%

profile of v1, /device:TPU:2, one launch (start us, length us, event | category | flops | bytes accessed | tf_op | source)
XLA Modules:
  0.0 170.9 jit_solution(9521124109590117961)
XLA Ops:
  6.5 0.0 all-reduce.3.cloned.1.call-start
  6.5 4.3 %multiply_convert_fusion = (bf16[128,1,2048]{2,0,1:T(8,128)(2,1)S(1)}, bf16[128,1,2048]{2,0,1:T(8,128)(2,1)S(1)}) fusion(), kind=kLoop, calls=%fused_computation.12 | loop fusion | flops 4980736 | bytes 1048576 | tf_op jit(solution)/shard_map/convert.1
  10.9 0.1 pad_maximum_fusion
  11.0 1.1 copy.31
  12.1 0.4 convert_element_type.30
  12.5 3.5 %convolution_convert_fusion = bf16[256,1024]{1,0:T(8,128)(2,1)S(1)} fusion(bf16[256,2048]{1,0:T(8,128)(2,1)S(1)} %convert_element_type.30, bf16[1024,2048]{1,0:T(8,128)(2,1)} %bitcast.704), kind=kOutput, calls=%fused_computation.4 | convolution fusion | flops 1074003968 | bytes 5767168 | tf_op jit(solution)/shard_map/dot_general | solution.py:29
  16.0 0.4 reshape.179
  16.4 35.2 %all_to_all.33 = bf16[128,2,4,256]{3,2,1,0:T(4,128)(2,1)S(1)} all-to-all(bf16[128,2,4,256]{3,2,1,0:T(4,128)(2,1)S(1)} %reshape.179), channel_id=1, replica_groups=mesh['grp'=4,'wide'=128] {'wide'}, dimensions={0} | all-to-all | bytes 1048576 | tf_op jit(solution)/shard_map/all_to_all | solution.py:33
  51.6 0.5 copy.41
  52.0 0.5 convolution_bitcast_fusion
  52.6 1.0 copy.37
  53.6 0.0 all-reduce.3.cloned.1.call-update
  53.7 1.3 dynamic-slice
  55.6 59.9 %all-reduce.3.cloned.1.call-done = f32[1,2,256,256]{3,1,0,2:T(2,128)} async-done(((f32[1,2,256,256]{3,1,0,2:T(2,128)}), f32[1,2,256,256]{3,1,0,2:T(2,128)}) %all-reduce.3.cloned.1.call-update) | async-done | bytes 524304
  115.5 0.9 constant_dynamic-slice_fusion
  118.0 24.9 %all_to_all.34 = f32[128,1,2,128]{3,2,1,0:T(2,128)S(1)} all-to-all(f32[128,1,2,128]{3,2,1,0:T(2,128)S(1)} %constant_dynamic-update-slice_fusion), channel_id=1, replica_groups=mesh['grp'=4,'wide'=128] {'wide'}, dimensions={0} | all-to-all | bytes 262144 | tf_op jit(solution)/shard_map/all_to_all | solution.py:45
  142.9 0.1 fusion.16
  143.0 0.3 fusion.17
  143.3 0.3 fusion
  143.6 0.1 copy.38
  143.7 18.1 %all_to_all.35 = f32[128,1,128]{2,1,0:T(1,128)S(1)} all-to-all(f32[128,1,128]{2,1,0:T(1,128)S(1)} %copy.38), channel_id=1, replica_groups=mesh['grp'=4,'wide'=128] {'wide'}, dimensions={0} | all-to-all | bytes 131072 | tf_op jit(solution)/shard_map/all_to_all | solution.py:49
  161.8 0.5 broadcast.137
  162.4 0.8 reduce.3
  163.2 0.8 convolution_bitcast_fusion.1
  (138 shorter events, 1.3 us)
Async XLA Ops:
  6.5 156.7 %copy-start = (f32[1,256,128]{2,1,0:T(8,128)S(1)}, f32[1,256,128]{2,1,0:T(8,128)}, u32[]{:S(2)}) copy-start(f32[1,256,128]{2,1,0:T(8,128)} %param.7) | copy-start | bytes 393220
  6.5 109.0 %all-reduce.3.cloned.1.call-start = ((), (), s32[]{:S(2)}) async-start(), calls=%async_computation.3 | async-start | bytes 1048576
  51.6 91.4 %copy-start.1 = (f32[128,128]{1,0:T(8,128)S(1)}, f32[128,128]{1,0:T(8,128)}, u32[]{:S(2)}) copy-start(f32[128,128]{1,0:T(8,128)} %param.5) | copy-start | bytes 196612
  51.6 91.7 %copy-start.2 = (f32[128,128]{1,0:T(8,128)S(1)}, f32[128,128]{1,0:T(8,128)}, u32[]{:S(2)}) copy-start(f32[128,128]{1,0:T(8,128)} %param.6) | copy-start | bytes 196612
Sparse Core Ops, SparseCore 0:
  53.8 61.6 all-reduce.2
